TPU v7x, 32 devices: a whole 2x2x4 slice. The times are simulated.
32 devices in a mesh: emit: 4 (over z), elem: 8 (over y, x, core).
Axes of the slice: x: 2, y: 2, z: 4, core: 2. Of those that a mesh axis runs over, the one named last changes fastest.
Arguments:
- traces: float32 [256, 1024, 1024], P('emit', 'elem'), may hold values from -6 to 6
- codes: float32 [4, 2, 128], replicated, may hold values from -0.5 to 0.5
- code_of: int32 [256], replicated, may hold values from 0 to 3
- order: int32 [256], replicated, may hold values from 0 to 255, each once
- steer: float32 [256, 1024, 256], P(None, 'elem'), may hold values from -0.1875 to 0.1875
Outputs:
- beams: float32 [256, 256, 256], P('elem', 'emit')
Inputs may be any that keep to these rules, and one draw needn't show every extreme that they name: `order`: each value 0 to 255 appears exactly once.
All inputs are finite; a program needn't handle non-finite values.
Results may differ from a plain program's by a relative error of at most 0.000071.
Values sent between devices are 32-bit elements; how exact they have to be, the bound alone decides.
No kernel may reach another device: no remote copies, remote signals or barrier semaphores. Data moves between devices by JAX's collectives and lax.ppermute only.
A program may use at most 320 MiB of HBM per device.

v0:
```python
import jax
import jax.numpy as jnp
from jax import lax
from jax.sharding import PartitionSpec as P


def toeplitz_table(codes):
    taps = codes.shape[2]
    rows = jnp.arange(2 * taps, dtype=jnp.int32)[:, None]
    cols = jnp.arange(taps, dtype=jnp.int32)[None, :]
    offset = rows - cols
    inside = (offset >= 0) & (offset < taps)
    clipped = jnp.clip(offset, 0, taps - 1)
    in_phase = jnp.where(inside[None], codes[:, 0, :][:, clipped], 0.0)
    quadrature = jnp.where(inside[None], codes[:, 1, :][:, clipped], 0.0)
    return jnp.concatenate([in_phase, quadrature], axis=2)


def hadamard_signs(order, columns, emissions):
    parity = jnp.zeros((order.shape[0], columns.shape[0]), jnp.int32)
    for bit in range(emissions.bit_length()):
        parity = parity + (order[:, None] >> bit & columns[None, :] >> bit & 1)
    signs = (1 - 2 * (parity % 2)).astype(jnp.float32)
    return signs / jnp.sqrt(jnp.float32(emissions))


def spectral_table(samples, taps, bins):
    rows = jnp.arange(samples // taps * 2 * taps, dtype=jnp.int32)
    block = rows // (2 * taps)
    quad = rows // taps % 2
    sample = block * taps + rows % taps
    freqs = jnp.arange(bins, dtype=jnp.int32) - bins // 2
    phase = jnp.mod(sample[:, None] * freqs[None, :], samples).astype(jnp.float32)
    angle = phase * (2.0 * jnp.pi / samples)
    cosine = jnp.cos(angle)
    sine = jnp.sin(angle)
    is_quad = quad[:, None] == 1
    real_cols = jnp.where(is_quad, sine, cosine)
    imag_cols = jnp.where(is_quad, cosine, -sine)
    return jnp.concatenate([real_cols, imag_cols], axis=1) / jnp.sqrt(jnp.float32(samples))


def steer_bins(source, steer, count, contract):
    bins = steer.shape[0]
    half = steer.shape[2] // 2
    real_part = lax.slice_in_dim(source, 0, count, axis=0)
    imag_part = lax.dynamic_slice_in_dim(source, bins, count, 0)
    numbers = (((contract,), (1,)), ((0,), (0,)))
    first = lax.dot_general(real_part, steer, numbers, precision=lax.Precision.HIGHEST)
    second = lax.dot_general(imag_part, steer, numbers, precision=lax.Precision.HIGHEST)
    return jnp.concatenate(
        [first[..., :half] - second[..., half:], first[..., half:] + second[..., :half]], axis=2
    )


def per_device(traces, codes, code_of, order, steer):
    edev, mdev, samples = traces.shape
    ncode, taps = (codes.shape[0], codes.shape[2])
    emissions = order.shape[0]
    bins = steer.shape[0]
    bins_dev = bins // lax.axis_size("elem")
    nblock = samples // taps
    first = lax.axis_index("emit") * edev
    own_codes = lax.dynamic_slice_in_dim(code_of, first, edev)
    onehot = (own_codes[:, None] == jnp.arange(ncode, dtype=jnp.int32)[None, :]).astype(jnp.float32)
    table = toeplitz_table(codes)
    picked = jnp.einsum("ec,cjd->ejd", onehot, table, precision=lax.Precision.HIGHEST)
    blocks = traces.reshape(edev, mdev, nblock, taps)
    current = jnp.einsum(
        "emnj,ejd->emnd", blocks, picked[:, :taps, :], precision=lax.Precision.HIGHEST
    )
    following = jnp.einsum(
        "emnj,ejd->emnd", blocks, picked[:, taps:, :], precision=lax.Precision.HIGHEST
    )
    following = jnp.concatenate(
        [following[:, :, 1:], jnp.zeros((edev, mdev, 1, 2 * taps), jnp.float32)], axis=2
    )
    corr = (current + following).reshape(edev, mdev, nblock * 2 * taps)
    transform = spectral_table(samples, taps, bins)
    spectra = lax.dot_general(
        transform, corr, (((0,), (2,)), ((), ())), precision=lax.Precision.HIGHEST
    )
    columns = first + jnp.arange(edev, dtype=jnp.int32)
    hadamard = hadamard_signs(order, columns, emissions)
    coded = lax.psum_scatter(
        steer_bins(spectra, steer, bins_dev * lax.axis_size("elem"), 2),
        "elem",
        scatter_dimension=0,
        tiled=True,
    )
    folded = lax.dot_general(
        lax.all_gather(coded, "emit", axis=1, tiled=True),
        hadamard,
        (((1,), (0,)), ((), ())),
        precision=lax.Precision.HIGHEST,
    )
    beams = jnp.transpose(folded, (0, 2, 1))
    return beams


def solution(mesh):
    placed = (P("emit", "elem", None), P(), P(), P(), P(None, "elem", None))
    return jax.shard_map(
        per_device, mesh=mesh, in_specs=placed, out_specs=P("elem", "emit", None), check_vma=False
    )
```

profile of v0, /device:TPU:0, one launch (start us, length us, event | category | flops | bytes accessed | tf_op | source)
XLA Modules:
  0.0 971.7 jit_solution(796748638702718246)
XLA Ops:
  6.5 0.0 reduce-scatter.2.cloned.1.call-start
  6.5 0.1 fusion.34
  6.7 0.8 fusion.103
  7.5 0.1 copy.39
  7.6 109.0 %gather_fusion = f32[32768,4]{1,0:T(8,128)} fusion(f32[4,128]{0,1:T(8,128)S(1)} %bitcast.66, s32[32768]{0:T(1024)S(1)} %fusion.34), kind=kCustom, calls=%fused_computation | custom fusion | bytes 1179648 | tf_op jit(solution)/shard_map/gather | solution.py:14
  116.5 9.4 copy.17
  126.0 0.1 copy.40
  126.1 109.0 %gather_fusion.1 = f32[32768,4]{1,0:T(8,128)} fusion(f32[4,128]{0,1:T(8,128)S(1)} %bitcast.65, s32[32768]{0:T(1024)S(1)} %fusion.34), kind=kCustom, calls=%fused_computation.1 | custom fusion | bytes 1179648 | tf_op jit(solution)/shard_map/gather | solution.py:15
  235.0 0.0 copy-start.1
  235.0 9.4 copy.20
  244.5 0.0 copy-done.1
  244.5 0.1 dynamic_slice.6
  244.6 0.3 select_bitcast_fusion.1
  244.9 7.0 fusion.26
  251.9 6.4 slice_bitcast_fusion.1
  258.3 65.5 %fusion.8 = f32[64,128,8,256]{1,3,2,0:T(8,128)} fusion(f32[64,128,256,1]{2,0,1,3:T(8,128)} %get-tuple-element.10, f32[64,128,1024]{2,1,0:T(8,128)} %param.5), kind=kOutput, calls=%fused_computation.9 | convolution fusion | flops 25769803776 | bytes 109051904 | tf_op jit(solution)/shard_map/emnj,ejd->emnd/dot_general | solution.py:72
  323.8 38.4 %slice.46 = f32[64,128,7,256]{1,3,2,0:T(8,128)} slice(f32[64,128,8,256]{1,3,2,0:T(8,128)} %fusion.8), slice={[0:64], [0:128], [1:8], [0:256]} | slice | bytes 117440512 | tf_op jit(solution)/shard_map/slice | solution.py:76
  362.2 88.9 %bitcast_add_fusion = f32[64,128,8,256]{1,3,2,0:T(8,128)} fusion(f32[64,128,7,256]{1,3,2,0:T(8,128)} %slice.46, f32[64,128,256,1]{2,0,1,3:T(8,128)} %get-tuple-element.9, f32[64,128,1024]{2,1,0:T(8,128)} %param.5), kind=kOutput, calls=%fused_computation.2 | convolution fusion | flops 25786580992 | bytes 167772160 | tf_op jit(solution)/shard_map/emnj,ejd->emnd/dot_general | solution.py:69
  451.1 8.4 fusion.32
  459.5 113.8 %fusion.18 = f32[512,64,128]{2,0,1:T(8,128)} fusion(f32[64,128,2048]{1,2,0:T(8,128)} %bitcast.13, f32[2048,256]{0,1:T(8,128)S(1)} %get-tuple-element.14, f32[2048,256]{0,1:T(8,128)S(1)} %get-tuple-element.13), kind=kOutput, calls=%fused_computation.23 | convolution fusion | flops 103081312256 | bytes 88080384 | tf_op jit(solution)/shard_map/dot_general | solution.py:80
  573.3 11.1 %fusion.102 = (f32[256,64,128]{2,0,1:T(8,128)}, f32[256,64,128]{2,0,1:T(8,128)}) fusion(f32[512,64,128]{2,0,1:T(8,128)} %fusion.18), kind=kLoop, calls=%fused_computation.140 | loop fusion | bytes 33554432 | tf_op jit(solution)/shard_map/slice | solution.py:46
  584.4 34.5 %fusion.13 = f32[256,64,256]{2,1,0:T(8,128)} fusion(f32[256,128,256]{2,1,0:T(8,128)} %param.9, f32[256,64,128]{2,0,1:T(8,128)} %get-tuple-element.8), kind=kOutput, calls=%fused_computation.17 | convolution fusion | flops 6442450944 | bytes 58720256 | tf_op jit(solution)/shard_map/dot_general | solution.py:50
  618.9 34.9 %fusion.15 = f32[256,64,256]{2,1,0:T(8,128)} fusion(f32[256,128,256]{2,1,0:T(8,128)} %param.9, f32[256,64,128]{2,0,1:T(8,128)} %get-tuple-element.7), kind=kOutput, calls=%fused_computation.19 | convolution fusion | flops 6442450944 | bytes 58720256 | tf_op jit(solution)/shard_map/dot_general | solution.py:49
  653.9 18.7 %slice_subtract_fusion = (f32[256,64,128]{2,1,0:T(8,128)}, f32[256,64,128]{2,1,0:T(8,128)}) fusion(f32[256,64,256]{2,1,0:T(8,128)} %fusion.13, f32[256,64,256]{2,1,0:T(8,128)} %fusion.15), kind=kLoop, calls=%fused_computation.12 | loop fusion | flops 4194304 | bytes 50331648 | tf_op jit(solution)/shard_map/sub | solution.py:52
  672.6 11.5 %pad_maximum_fusion = f32[256,64,256]{2,1,0:T(8,128)} fusion(f32[256,64,128]{2,1,0:T(8,128)} %get-tuple-element.6, f32[256,64,128]{2,1,0:T(8,128)} %get-tuple-element.5), kind=kLoop, calls=%fused_computation.10 | loop fusion | flops 4194304 | bytes 33554432 | tf_op jit(solution)/shard_map/concatenate | solution.py:51
  684.1 0.0 copy-start
  684.1 0.0 reduce-scatter.2.cloned.1.call-update
  684.1 0.2 all-gather.2.cloned.1.call-start
  684.3 118.8 %reduce-scatter.2.cloned.1.call-done = f32[32,64,256]{2,1,0:T(8,128)} async-done(((f32[256,64,256]{2,1,0:T(8,128)}), f32[32,64,256]{2,1,0:T(8,128)}) %reduce-scatter.2.cloned.1.call-update) | async-done | bytes 2097168 | tf_op jit(solution)/shard_map/reduce_scatter | solution.py:85
  803.2 0.0 all-gather.2.cloned.1.call-update
  803.2 0.0 copy-done
  803.3 151.1 %all-gather.2.cloned.1.call-done = f32[32,256,256]{2,1,0:T(8,128)} async-done(((f32[32,64,256]{2,1,0:T(8,128)}), f32[32,256,256]{2,1,0:T(8,128)}) %all-gather.2.cloned.1.call-update) | async-done | bytes 8388624 | tf_op jit(solution)/shard_map/all_gather | solution.py:92
  954.4 10.3 %convolution_bitcast_fusion = f32[32,64,256]{2,1,0:T(8,128)} fusion(f32[32,256,256]{2,1,0:T(8,128)} %all-gather.2.cloned.1.call-done, s32[64]{0:T(128)S(1)} %get-tuple-element.26, s32[256]{0:T(256)S(1)} %get-tuple-element.24, s32[64]{0:T(128)S(1)} %get-tuple-element.27, s32[256]{0:T(256)S(1)} %get-tuple-element.25, s32[64]{0:T(128)S(1)} %get-tuple-element.28, ...), kind=kOutput, calls=%fused_computation.36 | convolution fusion | flops 1611284480 | bytes 10497280 | tf_op jit(solution)/shard_map/dot_general | solution.py:91
  (10 shorter events, 0.1 us)
Async XLA Ops:
  6.5 796.6 %reduce-scatter.2.cloned.1.call-start = ((), (), s32[]{:S(2)}) async-start(), calls=%async_computation.1 | async-start | bytes 18874368 | tf_op jit(solution)/shard_map/reduce_scatter | solution.py:85
  235.0 9.4 copy-start.1
  684.1 119.2 %copy-start = (s32[256]{0:T(256)S(1)}, s32[256]{0:T(256)}, u32[]{:S(2)}) copy-start(s32[256]{0:T(256)} %param.8) | copy-start | bytes 3076
  684.1 270.3 %all-gather.2.cloned.1.call-start = ((), (), s32[]{:S(2)}) async-start(), calls=%async_computation.2 | async-start | bytes 10485760 | tf_op jit(solution)/shard_map/all_gather | solution.py:92
Sparse Core Ops, SparseCore 0:
  684.2 118.8 reduce-scatter.1
  804.7 149.6 all-gather.1
where the time goes:
time: 979 us; the launch traced here: 972 us
  matrix products  355 us (36%)
  local copies, waits for them, and re-layouts  294 us (30%)
  waiting for transfers between devices  270 us (28%)
  other arithmetic  39.1 us (4%)
  between operations  13.7 us (1%)
    all_gather x1, waiting for transfers between devices, per_device(): lax.all_gather(coded, 'emit', axis=1, tiled=True)  151 us
    reduce_scatter x1, waiting for transfers between devices, per_device(): lax.psum_scatter(steer_bins(spectra, steer, bins_dev * lax.axis_size('ele...  119 us
    gather x2, local copies, waits for them, and re-layouts, toeplitz_table(): quadrature = jnp.where(inside[None], codes[:, 1, :][:, clipped], 0.0)  118 us
    gather x2, local copies, waits for them, and re-layouts, toeplitz_table(): in_phase = jnp.where(inside[None], codes[:, 0, :][:, clipped], 0.0)  118 us
    dot_general x1, matrix products, per_device(): lax.dot_general(transform, corr, (((0,), (2,)), ((), ())), precision=lax....  114 us
    dot_general x1, matrix products, per_device(): jnp.einsum('emnj,ejd->emnd', blocks, picked[:, :taps, :], precision=lax.P...  88.9 us
    dot_general x1, matrix products, per_device(): jnp.einsum('emnj,ejd->emnd', blocks, picked[:, taps:, :], precision=lax.P...  65.5 us
    slice x1, local copies, waits for them, and re-layouts, per_device(): following[:, :, 1:]  38.4 us
  transfers between devices with their start and end apart: 2, of which 2 were waited for; matrix products, arithmetic and copies ran while one was open for 0% of the time, Pallas kernels for 0%

commit v1 on v0

--- a/solution.py
+++ b/solution.py
@@ -1,7 +1,19 @@
+import functools
 import jax
 import jax.numpy as jnp
 from jax import lax
 from jax.sharding import PartitionSpec as P
+
+
+def put_the_slabs(arr, on_dim):
+    full_n = lax.axis_size("emit")
+    gallery = tuple((full_n if kk == on_dim else 1 for kk in range(arr.ndim)))
+    odd = jnp.tile(arr, gallery)
+    s_next = lax.all_to_all(odd, "emit", split_axis=on_dim, concat_axis=on_dim, tiled=True)
+    return s_next
+
+
+guide_the_tokens = functools.partial(put_the_slabs, on_dim=1)
 
 
 def toeplitz_table(codes):
@@ -89,10 +101,7 @@
         tiled=True,
     )
     folded = lax.dot_general(
-        lax.all_gather(coded, "emit", axis=1, tiled=True),
-        hadamard,
-        (((1,), (0,)), ((), ())),
-        precision=lax.Precision.HIGHEST,
+        guide_the_tokens(coded), hadamard, (((1,), (0,)), ((), ())), precision=lax.Precision.HIGHEST
     )
     beams = jnp.transpose(folded, (0, 2, 1))
     return beams

time: 979 us -> 1030 us (1.052)
  waiting for transfers between devices: 270 us -> 302 us
    all_to_all x0 -> x1, waiting for transfers between devices: none -> 183 us  [put_the_slabs(): lax.all_to_all(odd, 'emit', split_axis=on_dim, concat_axis=on_dim, tiled=...]
    all_gather x1 -> x0, waiting for transfers between devices: 151 us -> none  [per_device(): lax.all_gather(coded, 'emit', axis=1, tiled=True)]
where the time goes in v1:
time: 1030 us; the launch traced here: 1020 us
  matrix products  359 us (35%)
  waiting for transfers between devices  302 us (29%)
  local copies, waits for them, and re-layouts  300 us (29%)
  other arithmetic  39.2 us (4%)
  between operations  13.7 us (1%)
    all_to_all x1, waiting for transfers between devices, put_the_slabs(): lax.all_to_all(odd, 'emit', split_axis=on_dim, concat_axis=on_dim, tiled=...  183 us
    reduce_scatter x1, waiting for transfers between devices, per_device(): lax.psum_scatter(steer_bins(spectra, steer, bins_dev * lax.axis_size('ele...  119 us
    gather x2, local copies, waits for them, and re-layouts, toeplitz_table(): quadrature = jnp.where(inside[None], codes[:, 1, :][:, clipped], 0.0)  118 us
    gather x2, local copies, waits for them, and re-layouts, toeplitz_table(): in_phase = jnp.where(inside[None], codes[:, 0, :][:, clipped], 0.0)  118 us
    dot_general x1, matrix products, per_device(): lax.dot_general(transform, corr, (((0,), (2,)), ((), ())), precision=lax....  114 us
    dot_general x1, matrix products, per_device(): jnp.einsum('emnj,ejd->emnd', blocks, picked[:, :taps, :], precision=lax.P...  88.7 us
    dot_general x1, matrix products, per_device(): jnp.einsum('emnj,ejd->emnd', blocks, picked[:, taps:, :], precision=lax.P...  65.5 us
    slice x1, local copies, waits for them, and re-layouts, per_device(): following[:, :, 1:]  38.4 us
  transfers between devices with their start and end apart: 2, of which 2 were waited for; matrix products, arithmetic and copies ran while one was open for 0% of the time, Pallas kernels for 0%

profile of v1, /device:TPU:0, one launch (start us, length us, event | category | flops | bytes accessed | tf_op | source)
XLA Modules:
  0.0 1019.4 jit_solution(5315561227958234504)
XLA Ops:
  6.5 0.0 reduce-scatter.2.cloned.1.call-start
  6.5 0.1 fusion.39
  6.7 0.8 fusion.108
  7.5 0.1 copy.54
  7.6 108.3 %gather_fusion = f32[32768,4]{1,0:T(8,128)} fusion(f32[4,128]{0,1:T(8,128)S(1)} %bitcast.66, s32[32768]{0:T(1024)S(1)} %fusion.39), kind=kCustom, calls=%fused_computation | custom fusion | bytes 1179648 | tf_op jit(solution)/shard_map/gather | solution.py:26
  115.9 9.4 copy.30
  125.3 0.1 copy.55
  125.4 108.3 %gather_fusion.1 = f32[32768,4]{1,0:T(8,128)} fusion(f32[4,128]{0,1:T(8,128)S(1)} %bitcast.65, s32[32768]{0:T(1024)S(1)} %fusion.39), kind=kCustom, calls=%fused_computation.1 | custom fusion | bytes 1179648 | tf_op jit(solution)/shard_map/gather | solution.py:27
  233.8 0.0 copy-start.1
  233.8 9.4 copy.33
  243.2 0.0 copy-done.1
  243.2 0.1 dynamic_slice.6
  243.3 0.3 select_bitcast_fusion.1
  243.6 7.0 fusion.31
  250.6 6.4 slice_bitcast_fusion.1
  257.0 65.5 %fusion.8 = f32[64,128,8,256]{1,3,2,0:T(8,128)} fusion(f32[64,128,256,1]{2,0,1,3:T(8,128)} %get-tuple-element.10, f32[64,128,1024]{2,1,0:T(8,128)} %param.5), kind=kOutput, calls=%fused_computation.9 | convolution fusion | flops 25769803776 | bytes 109051904 | tf_op jit(solution)/shard_map/emnj,ejd->emnd/dot_general | solution.py:84
  322.5 38.4 %slice.46 = f32[64,128,7,256]{1,3,2,0:T(8,128)} slice(f32[64,128,8,256]{1,3,2,0:T(8,128)} %fusion.8), slice={[0:64], [0:128], [1:8], [0:256]} | slice | bytes 117440512 | tf_op jit(solution)/shard_map/slice | solution.py:88
  360.9 88.7 %bitcast_add_fusion = f32[64,128,8,256]{1,3,2,0:T(8,128)} fusion(f32[64,128,7,256]{1,3,2,0:T(8,128)} %slice.46, f32[64,128,256,1]{2,0,1,3:T(8,128)} %get-tuple-element.9, f32[64,128,1024]{2,1,0:T(8,128)} %param.5), kind=kOutput, calls=%fused_computation.2 | convolution fusion | flops 25786580992 | bytes 167772160 | tf_op jit(solution)/shard_map/emnj,ejd->emnd/dot_general | solution.py:81
  449.6 8.4 fusion.37
  458.1 113.8 %fusion.20 = f32[512,64,128]{2,0,1:T(8,128)} fusion(f32[64,128,2048]{1,2,0:T(8,128)} %bitcast.13, f32[2048,256]{0,1:T(8,128)S(1)} %get-tuple-element.14, f32[2048,256]{0,1:T(8,128)S(1)} %get-tuple-element.13), kind=kOutput, calls=%fused_computation.25 | convolution fusion | flops 103081312256 | bytes 88080384 | tf_op jit(solution)/shard_map/dot_general | solution.py:92
  571.9 11.1 %fusion.107 = (f32[256,64,128]{2,0,1:T(8,128)}, f32[256,64,128]{2,0,1:T(8,128)}) fusion(f32[512,64,128]{2,0,1:T(8,128)} %fusion.20), kind=kLoop, calls=%fused_computation.142 | loop fusion | bytes 33554432 | tf_op jit(solution)/shard_map/slice | solution.py:58
  582.9 34.5 %fusion.15 = f32[256,64,256]{2,1,0:T(8,128)} fusion(f32[256,128,256]{2,1,0:T(8,128)} %param.9, f32[256,64,128]{2,0,1:T(8,128)} %get-tuple-element.8), kind=kOutput, calls=%fused_computation.19 | convolution fusion | flops 6442450944 | bytes 58720256 | tf_op jit(solution)/shard_map/dot_general | solution.py:62
  617.5 34.9 %fusion.17 = f32[256,64,256]{2,1,0:T(8,128)} fusion(f32[256,128,256]{2,1,0:T(8,128)} %param.9, f32[256,64,128]{2,0,1:T(8,128)} %get-tuple-element.7), kind=kOutput, calls=%fused_computation.21 | convolution fusion | flops 6442450944 | bytes 58720256 | tf_op jit(solution)/shard_map/dot_general | solution.py:61
  652.4 18.7 %slice_subtract_fusion = (f32[256,64,128]{2,1,0:T(8,128)}, f32[256,64,128]{2,1,0:T(8,128)}) fusion(f32[256,64,256]{2,1,0:T(8,128)} %fusion.15, f32[256,64,256]{2,1,0:T(8,128)} %fusion.17), kind=kLoop, calls=%fused_computation.12 | loop fusion | flops 4194304 | bytes 50331648 | tf_op jit(solution)/shard_map/sub | solution.py:64
  671.0 11.7 %pad_maximum_fusion = f32[256,64,256]{2,1,0:T(8,128)} fusion(f32[256,64,128]{2,1,0:T(8,128)} %get-tuple-element.6, f32[256,64,128]{2,1,0:T(8,128)} %get-tuple-element.5), kind=kLoop, calls=%fused_computation.10 | loop fusion | flops 4194304 | bytes 33554432 | tf_op jit(solution)/shard_map/concatenate | solution.py:63
  682.7 0.0 reduce-scatter.2.cloned.1.call-update
  682.7 119.1 %reduce-scatter.2.cloned.1.call-done = f32[32,64,256]{2,1,0:T(8,128)} async-done(((f32[256,64,256]{2,1,0:T(8,128)}), f32[32,64,256]{2,1,0:T(8,128)}) %reduce-scatter.2.cloned.1.call-update) | async-done | bytes 2097168 | tf_op jit(solution)/shard_map/reduce_scatter | solution.py:97
  801.8 2.8 copy.41
  804.6 4.3 tile.4
  808.9 0.0 copy-start
  808.9 5.8 all-to-all-start
  814.8 0.0 copy-done
  814.8 183.1 %all-to-all-done = f32[32,256,256]{2,0,1:T(8,128)} async-done(((f32[32,256,256]{2,0,1:T(8,128)}), f32[32,256,256]{2,0,1:T(8,128)}, u32[]{:S(2)}, u32[]{:S(2)}) %all-to-all-start) | async-done | bytes 8388640 | tf_op jit(solution)/shard_map/all_to_all | solution.py:12
  997.9 14.5 %fusion.28 = f32[32,64,256]{2,1,0:T(8,128)} fusion(f32[32,256,256]{2,0,1:T(8,128)} %all-to-all-done, s32[64]{0:T(128)S(1)} %get-tuple-element.26, s32[256]{0:T(256)S(1)} %get-tuple-element.24, s32[64]{0:T(128)S(1)} %get-tuple-element.27, s32[256]{0:T(256)S(1)} %get-tuple-element.25, s32[64]{0:T(128)S(1)} %get-tuple-element.28, ...), kind=kOutput, calls=%fused_computation.38 | convolution fusion | flops 1611284480 | bytes 10497280 | tf_op jit(solution)/shard_map/dot_general | solution.py:103
  (10 shorter events, 0.1 us)
Async XLA Ops:
  6.5 795.3 %reduce-scatter.2.cloned.1.call-start = ((), (), s32[]{:S(2)}) async-start(), calls=%async_computation.2 | async-start | bytes 18874368 | tf_op jit(solution)/shard_map/reduce_scatter | solution.py:97
  233.8 9.4 copy-start.1
  808.9 5.8 copy-start
  808.9 189.0 %all-to-all-start = ((f32[32,256,256]{2,0,1:T(8,128)}), f32[32,256,256]{2,0,1:T(8,128)}, u32[]{:S(2)}, u32[]{:S(2)}) async-start(f32[32,256,256]{2,0,1:T(8,128)} %bitcast.67), calls=%async_computation.1 | async-start | bytes 16777216 | tf_op jit(solution)/shard_map/all_to_all | solution.py:12
Sparse Core Ops, SparseCore 0:
  682.9 118.9 reduce-scatter.1
